TPU v7x, 32 devices: a whole 2x2x4 slice. The times are simulated.
32 devices in a mesh: dp: 16 (over z, y, x), mp: 2 (over core).
Axes of the slice: x: 2, y: 2, z: 4, core: 2. Of those that a mesh axis runs over, the one named last changes fastest.
Arguments:
- gradients: float32 [16, 4, 32, 8192], P('dp', None, 'mp'), may hold values from -6 to 6
- weights: float32 [4, 32, 8192], P(None, 'mp', 'dp'), may hold values from -40 to 40
- first_moment: float32 [4, 32, 8192], P(None, 'mp', 'dp'), may hold values from -0.6 to 0.6
- second_moment: float32 [4, 32, 8192], P(None, 'mp', 'dp'), may hold values from 0.001 to 0.1
- learn_rate: float32 [4], replicated, may hold values from 0.1 to 0.5
- weight_decay: float32 [4], replicated, may hold values from 0.1 to 1
Outputs:
- new_weights: float32 [4, 32, 8192], P(None, 'mp')
- new_first: float32 [4, 32, 8192], P(None, 'mp', 'dp')
- new_second: float32 [4, 32, 8192], P(None, 'mp', 'dp')
- trust_ratio: float32 [4], replicated
All inputs are finite; a program needn't handle non-finite values.
Results may differ from a plain program's by a relative error of at most 0.000062.
Values sent between devices are 32-bit elements; how exact they have to be, the bound alone decides.
No kernel may reach another device: no remote copies, remote signals or barrier semaphores. Data moves between devices by JAX's collectives and lax.ppermute only.
A program may use at most 64 MiB of HBM per device.

v0:
```python
import jax
import jax.numpy as jnp
from jax import lax
from jax.sharding import PartitionSpec as P

STEP = 10


def shards(gradients, weights, first_moment, second_moment, learn_rate, weight_decay):
    replicas = lax.axis_size("dp")
    summed = lax.psum_scatter(gradients, "dp", scatter_dimension=3, tiled=True)[0] * (
        1.0 / replicas
    )
    new_first = 0.9 * first_moment + 0.1 * summed
    new_second = 0.999 * second_moment + 0.001 * summed * summed
    first_fix = 1.0 - 0.9**STEP
    second_fix = 1.0 - 0.999**STEP
    update = (
        new_first / first_fix / (jnp.sqrt(new_second / second_fix) + 1e-06)
        + weight_decay[:, None, None] * weights
    )
    weight_sq, update_sq = lax.psum(
        (jnp.sum(weights * weights, axis=(1, 2)), jnp.sum(update * update, axis=(1, 2))),
        ("dp", "mp"),
    )
    trust_ratio = jnp.sqrt(weight_sq) / (jnp.sqrt(update_sq) + 1e-06)
    stepped = weights - (learn_rate * trust_ratio)[:, None, None] * update
    new_weights = lax.all_gather(stepped, "dp", axis=2, tiled=True)
    return (new_weights, new_first, new_second, trust_ratio)


def solution(mesh):
    in_specs = (
        P("dp", None, "mp", None),
        P(None, "mp", "dp"),
        P(None, "mp", "dp"),
        P(None, "mp", "dp"),
        P(),
        P(),
    )
    out_specs = (P(None, "mp", None), P(None, "mp", "dp"), P(None, "mp", "dp"), P())
    return jax.shard_map(shards, mesh=mesh, in_specs=in_specs, out_specs=out_specs, check_vma=False)
```

profile of v0, /device:TPU:0, one launch (start us, length us, event | category | flops | bytes accessed | tf_op | source)
XLA Modules:
  0.0 205.5 jit_solution(638651230014546051)
XLA Ops:
  7.2 0.0 copy-start
  7.2 0.0 copy-start.3
  7.2 0.0 copy-start.2
  7.2 0.0 copy-start.1
  7.2 0.0 copy-start.4
  7.2 0.0 reduce-scatter.2.cloned.1.call-start
  7.3 0.7 reduce-scatter.2.cloned.1.call-update
  7.9 0.0 all-gather.2.cloned.1.call-start
  8.0 86.7 %reduce-scatter.2.cloned.1.call-done = f32[1,4,16,512]{3,2,1,0:T(8,128)} async-done(((f32[1,4,16,8192]{3,2,1,0:T(8,128)}), f32[1,4,16,512]{3,2,1,0:T(8,128)}) %reduce-scatter.2.cloned.1.call-update) | async-done | bytes 131088 | tf_op jit(solution)/shard_map/reduce_scatter | solution.py:11
  94.7 0.0 copy-done
  94.7 0.0 copy-done.3
  94.7 0.0 copy-done.2
  94.7 0.0 copy-done.1
  94.7 1.7 multiply_reduce_fusion
  96.4 36.8 %all-reduce = (f32[4]{0:T(128)S(1)}, f32[4]{0:T(128)S(1)}) all-reduce(f32[4]{0:T(128)S(1)} %get-tuple-element.8, f32[4]{0:T(128)S(1)} %get-tuple-element.12), channel_id=1, replica_groups=mesh['dp'=16,'mp'=2] {'dp','mp'}, use_global_device_ids=true, to_apply=%region_4.0 | all-reduce | flops 8 | bytes 64 | tf_op jit(solution)/shard_map/psum | solution.py:22
  133.2 0.0 copy-done.4
  133.2 0.5 fusion
  133.7 0.7 multiply_subtract_fusion
  134.4 0.0 all-gather.2.cloned.1.call-update
  134.5 61.1 %all-gather.2.cloned.1.call-done = f32[4,16,8192]{2,1,0:T(8,128)} async-done(((f32[4,16,512]{2,1,0:T(8,128)}), f32[4,16,8192]{2,1,0:T(8,128)}) %all-gather.2.cloned.1.call-update) | async-done | bytes 2097168 | tf_op jit(solution)/shard_map/all_gather | solution.py:28
  195.6 3.1 %copy.11 = f32[4,16,8192]{2,1,0:T(8,128)} copy(f32[4,16,8192]{2,1,0:T(8,128)} %all-gather.2.cloned.1.call-done) | data formatting | bytes 4194304
Async XLA Ops:
  7.2 87.5 %copy-start = (f32[4,16,512]{2,1,0:T(8,128)S(1)}, f32[4,16,512]{2,1,0:T(8,128)}, u32[]{:S(2)}) copy-start(f32[4,16,512]{2,1,0:T(8,128)} %param.7) | copy-start | bytes 393220
  7.2 87.5 %copy-start.3 = (f32[4]{0:T(128)S(1)}, f32[4]{0:T(128)}, u32[]{:S(2)}) copy-start(f32[4]{0:T(128)} %param.11) | copy-start | bytes 52
  7.2 87.5 %copy-start.2 = (f32[4,16,512]{2,1,0:T(8,128)S(1)}, f32[4,16,512]{2,1,0:T(8,128)}, u32[]{:S(2)}) copy-start(f32[4,16,512]{2,1,0:T(8,128)} %param.9) | copy-start | bytes 393220
  7.2 87.5 %copy-start.1 = (f32[4,16,512]{2,1,0:T(8,128)S(1)}, f32[4,16,512]{2,1,0:T(8,128)}, u32[]{:S(2)}) copy-start(f32[4,16,512]{2,1,0:T(8,128)} %param.8) | copy-start | bytes 393220
  7.2 126.0 %copy-start.4 = (f32[4]{0:T(128)S(1)}, f32[4]{0:T(128)}, u32[]{:S(2)}) copy-start(f32[4]{0:T(128)} %param.10) | copy-start | bytes 52
  7.2 87.4 %reduce-scatter.2.cloned.1.call-start = ((), (), s32[]{:S(2)}) async-start(), calls=%async_computation.1 | async-start | bytes 2228224 | tf_op jit(solution)/shard_map/reduce_scatter | solution.py:11
  7.9 187.6 %all-gather.2.cloned.1.call-start = ((), (), s32[]{:S(2)}) async-start(), calls=%async_computation.2 | async-start | bytes 2228224 | tf_op jit(solution)/shard_map/all_gather | solution.py:28
Sparse Core Ops, SparseCore 0:
  10.3 84.3 reduce-scatter.1
  134.6 60.9 all-gather.1
where the time goes:
time: 206 us; the launch traced here: 205 us
  waiting for transfers between devices  148 us (72%)
  blocking collectives  36.8 us (18%)
  between operations  14.1 us (7%)
  local copies, waits for them, and re-layouts  3.08 us (1%)
  other arithmetic  2.97 us (1%)
    reduce_scatter x1, waiting for transfers between devices, shards(): lax.psum_scatter(gradients, 'dp', scatter_dimension=3, tiled=True)[0]  86.7 us
    all_gather x1, waiting for transfers between devices, shards(): new_weights = lax.all_gather(stepped, 'dp', axis=2, tiled=True)  61.1 us
    psum x1, blocking collectives, shards(): lax.psum((jnp.sum(weights * weights, axis=(1, 2)), jnp.sum(update * updat...  36.8 us
  transfers between devices with their start and end apart: 2, of which 2 were waited for; matrix products, arithmetic and copies ran while one was open for 0% of the time, Pallas kernels for 0%

commit v1 on v0

--- a/solution.py
+++ b/solution.py
@@ -20,8 +20,10 @@
         + weight_decay[:, None, None] * weights
     )
     weight_sq, update_sq = lax.psum(
-        (jnp.sum(weights * weights, axis=(1, 2)), jnp.sum(update * update, axis=(1, 2))),
-        ("dp", "mp"),
+        lax.psum(
+            (jnp.sum(weights * weights, axis=(1, 2)), jnp.sum(update * update, axis=(1, 2))), "mp"
+        ),
+        "dp",
     )
     trust_ratio = jnp.sqrt(weight_sq) / (jnp.sqrt(update_sq) + 1e-06)
     stepped = weights - (learn_rate * trust_ratio)[:, None, None] * update

time: 206 us -> 205 us (level)
  waiting for transfers between devices: 148 us -> 145 us
  blocking collectives: 36.8 us -> 39.6 us
    psum x0 -> x1, blocking collectives: none -> 37.1 us  [shards(): lax.psum(lax.psum((jnp.sum(weights * weights, axis=(1, 2)), jnp.sum(updat...]
    psum x1, blocking collectives: 36.8 us -> 2.45 us  [shards(): lax.psum((jnp.sum(weights * weights, axis=(1, 2)), jnp.sum(update * updat...]
    all_gather x1, waiting for transfers between devices: 61.1 us -> 57.9 us  [shards(): new_weights = lax.all_gather(stepped, 'dp', axis=2, tiled=True)]
where the time goes in v1:
time: 205 us
  waiting for transfers between devices  145 us (71%)
  blocking collectives  39.6 us (19%)
  between operations  14.1 us (7%)
  local copies, waits for them, and re-layouts  3.08 us (2%)
  other arithmetic  2.97 us (1%)
    reduce_scatter x1, waiting for transfers between devices, shards(): lax.psum_scatter(gradients, 'dp', scatter_dimension=3, tiled=True)[0]  86.7 us
    all_gather x1, waiting for transfers between devices, shards(): new_weights = lax.all_gather(stepped, 'dp', axis=2, tiled=True)  57.9 us
    psum x1, blocking collectives, shards(): lax.psum(lax.psum((jnp.sum(weights * weights, axis=(1, 2)), jnp.sum(updat...  37.1 us
  transfers between devices with their start and end apart: 2, of which 2 were waited for; matrix products, arithmetic and copies ran while one was open for 0% of the time, Pallas kernels for 0%

profile of v1, /device:TPU:0, one launch (start us, length us, event | category | flops | bytes accessed | tf_op | source)
XLA Modules:
  0.0 205.1 jit_solution(5192132023119095114)
XLA Ops:
  7.2 0.0 copy-start
  7.2 0.0 copy-start.3
  7.2 0.0 copy-start.2
  7.2 0.0 copy-start.1
  7.2 0.0 copy-start.4
  7.2 0.0 reduce-scatter.2.cloned.1.call-start
  7.3 0.7 reduce-scatter.2.cloned.1.call-update
  7.9 0.0 all-gather.2.cloned.1.call-start
  8.0 86.7 %reduce-scatter.2.cloned.1.call-done = f32[1,4,16,512]{3,2,1,0:T(8,128)} async-done(((f32[1,4,16,8192]{3,2,1,0:T(8,128)}), f32[1,4,16,512]{3,2,1,0:T(8,128)}) %reduce-scatter.2.cloned.1.call-update) | async-done | bytes 131088 | tf_op jit(solution)/shard_map/reduce_scatter | solution.py:11
  94.7 0.0 copy-done
  94.7 0.0 copy-done.3
  94.7 0.0 copy-done.2
  94.7 0.0 copy-done.1
  94.7 1.7 multiply_reduce_fusion
  96.4 2.4 %all-reduce.1 = (f32[4]{0:T(128)S(1)}, f32[4]{0:T(128)S(1)}) all-reduce(f32[4]{0:T(128)S(1)} %get-tuple-element.10, f32[4]{0:T(128)S(1)} %get-tuple-element.14), channel_id=1, replica_groups=mesh['dp'=16,'mp'=2] {'mp'}, use_global_device_ids=true, to_apply=%region_5.0 | all-reduce | flops 8 | bytes 64 | tf_op jit(solution)/shard_map/psum | solution.py:23
  98.8 37.1 %all-reduce = (f32[4]{0:T(128)S(1)}, f32[4]{0:T(128)S(1)}) all-reduce(f32[4]{0:T(128)S(1)} %get-tuple-element.6, f32[4]{0:T(128)S(1)} %get-tuple-element.7), channel_id=1, replica_groups=mesh['dp'=16,'mp'=2] {'dp'}, use_global_device_ids=true, to_apply=%region_6.0 | all-reduce | flops 8 | bytes 64 | tf_op jit(solution)/shard_map/psum | solution.py:22
  136.0 0.0 copy-done.4
  136.0 0.5 fusion
  136.5 0.7 multiply_subtract_fusion
  137.2 0.0 all-gather.2.cloned.1.call-update
  137.3 57.9 %all-gather.2.cloned.1.call-done = f32[4,16,8192]{2,1,0:T(8,128)} async-done(((f32[4,16,512]{2,1,0:T(8,128)}), f32[4,16,8192]{2,1,0:T(8,128)}) %all-gather.2.cloned.1.call-update) | async-done | bytes 2097168 | tf_op jit(solution)/shard_map/all_gather | solution.py:30
  195.2 3.1 %copy.11 = f32[4,16,8192]{2,1,0:T(8,128)} copy(f32[4,16,8192]{2,1,0:T(8,128)} %all-gather.2.cloned.1.call-done) | data formatting | bytes 4194304
Async XLA Ops:
  7.2 87.5 %copy-start = (f32[4,16,512]{2,1,0:T(8,128)S(1)}, f32[4,16,512]{2,1,0:T(8,128)}, u32[]{:S(2)}) copy-start(f32[4,16,512]{2,1,0:T(8,128)} %param.7) | copy-start | bytes 393220
  7.2 87.5 %copy-start.3 = (f32[4]{0:T(128)S(1)}, f32[4]{0:T(128)}, u32[]{:S(2)}) copy-start(f32[4]{0:T(128)} %param.11) | copy-start | bytes 52
  7.2 87.5 %copy-start.2 = (f32[4,16,512]{2,1,0:T(8,128)S(1)}, f32[4,16,512]{2,1,0:T(8,128)}, u32[]{:S(2)}) copy-start(f32[4,16,512]{2,1,0:T(8,128)} %param.9) | copy-start | bytes 393220
  7.2 87.5 %copy-start.1 = (f32[4,16,512]{2,1,0:T(8,128)S(1)}, f32[4,16,512]{2,1,0:T(8,128)}, u32[]{:S(2)}) copy-start(f32[4,16,512]{2,1,0:T(8,128)} %param.8) | copy-start | bytes 393220
  7.2 128.8 %copy-start.4 = (f32[4]{0:T(128)S(1)}, f32[4]{0:T(128)}, u32[]{:S(2)}) copy-start(f32[4]{0:T(128)} %param.10) | copy-start | bytes 52
  7.2 87.4 %reduce-scatter.2.cloned.1.call-start = ((), (), s32[]{:S(2)}) async-start(), calls=%async_computation.1 | async-start | bytes 2228224 | tf_op jit(solution)/shard_map/reduce_scatter | solution.py:11
  7.9 187.2 %all-gather.2.cloned.1.call-start = ((), (), s32[]{:S(2)}) async-start(), calls=%async_computation.2 | async-start | bytes 2228224 | tf_op jit(solution)/shard_map/all_gather | solution.py:30
Sparse Core Ops, SparseCore 0:
  10.3 84.3 reduce-scatter.1
  137.4 57.7 all-gather.1
